TPU v7x, 32 devices: a whole 2x2x4 slice. The times are simulated.
32 devices in a mesh: seq: 8 (over y, x, core), mp: 4 (over z).
Axes of the slice: x: 2, y: 2, z: 4, core: 2. Of those that a mesh axis runs over, the one named last changes fastest.
Arguments:
- tokens: bfloat16 [1024, 4096], P('seq', 'mp'), may hold values from -10 to 10
- norm_gain: float32 [4096], replicated, may hold values from 0.1 to 1.9
- w_cand: bfloat16 [4096, 4096], P('seq', 'mp'), may hold values from -0.125 to 0.125
- w_gate: bfloat16 [4096, 4096], P('seq', 'mp'), may hold values from -0.046875 to 0.046875
- rec_gate: float32 [4096], P('mp'), may hold values from -0.75 to 0.75
- rec_cand: float32 [4096], P('mp'), may hold values from -0.6 to 0.6
- bias_gate: float32 [4096], P('mp')
- w_out: bfloat16 [4096, 4096], P('mp'), may hold values from -0.09375 to 0.09375
Outputs:
- output: bfloat16 [1024, 4096], P('seq', 'mp')
All inputs are finite; a program needn't handle non-finite values.
Results may differ from a plain program's by a relative error of at most 0.0048.
Values may be sent and summed in bfloat16 or wider, within the bound.
A program may use at most 64 MiB of HBM per device.

v0:
```python
import functools

import jax
import jax.numpy as jnp
from jax import lax
from jax.experimental import pallas as pl
from jax.experimental.pallas import tpu as pltpu
from jax.sharding import PartitionSpec as P

NEWTON = 3


def prefix(value, axis, join, neutral):
    count, mine = (lax.axis_size(axis), lax.axis_index(axis))
    pieces = jax.tree.map(lambda part: lax.all_gather(part, axis), value)
    subtotal = jax.tree.map(
        lambda part, zero: jnp.full_like(part, 0) + jnp.asarray(zero, part.dtype), value, neutral
    )

    def lap(position, subtotal):
        longer = join(subtotal, jax.tree.map(lambda part: part[position], pieces))
        return jax.tree.map(lambda new, old: jnp.where(position < mine, new, old), longer, subtotal)

    return lax.fori_loop(0, count - 1, lap, subtotal)


def compose(earlier, later):
    return (later[0] * earlier[0], later[0] * earlier[1] + later[1])


def cell(previous, cand_pre, gate_pre, rec_gate, rec_cand, bias_gate):
    gate = jax.nn.sigmoid(gate_pre + rec_gate * previous + bias_gate)
    cand = jnp.tanh(cand_pre + rec_cand * previous)
    value = gate * previous + (1.0 - gate) * cand
    slope = (
        gate
        + gate * (1.0 - gate) * rec_gate * (previous - cand)
        + (1.0 - gate) * (1.0 - cand * cand) * rec_cand
    )
    return (value, slope)


def per_device(tokens, norm_gain, w_cand, w_gate, rec_gate, rec_cand, bias_gate, w_out):
    tok_rows = tokens.shape[0]
    channels = w_cand.shape[1]
    whole = lax.all_gather(tokens, "mp", axis=1, tiled=True)
    wide = whole.astype(jnp.float32)
    factor = lax.rsqrt(jnp.mean(wide * wide, axis=1, keepdims=True) + 1e-05)
    normed = (wide * factor * norm_gain).astype(jnp.bfloat16)
    cand_pre = jnp.dot(
        normed,
        lax.all_gather(w_cand, "seq", axis=0, tiled=True),
        preferred_element_type=jnp.float32,
    )
    gate_pre = jnp.dot(
        normed,
        lax.all_gather(w_gate, "seq", axis=0, tiled=True),
        preferred_element_type=jnp.float32,
    )
    state = jnp.zeros((tok_rows, channels), jnp.float32)
    carried = jnp.zeros((channels,), jnp.float32)
    ones_row = jnp.ones((channels,), jnp.float32)
    for newton_step in range(NEWTON):
        previous = jnp.concatenate([carried[None, :], state[:-1]], axis=0)
        value, slope = cell(previous, cand_pre, gate_pre, rec_gate, rec_cand, bias_gate)
        offset = value - slope * previous
        sweep_a, sweep_b = lax.associative_scan(compose, (slope, offset), axis=0)
        entering = prefix((sweep_a[-1], sweep_b[-1]), "seq", compose, (ones_row, carried * 0.0))
        carried = entering[1]
        state = sweep_a * carried + sweep_b
    state_b = state.astype(jnp.bfloat16)
    partial_sums = jnp.dot(state_b, w_out, preferred_element_type=jnp.float32)
    summed = lax.psum_scatter(partial_sums, "mp", scatter_dimension=1, tiled=True)
    return summed.astype(jnp.bfloat16)


CORES = 2
SUBLANES = 8
LANES = 128
PIECES = 8
HALVES = 2
GROUP = 16
MESH = pl.DeviceIdType.MESH


def fused_kernel(
    n_seq,
    n_mp,
    tok_ref,
    gain_ref,
    wc_hbm,
    wg_hbm,
    rg_ref,
    rc_ref,
    bg_ref,
    wo_hbm,
    out_ref,
    raw,
    xk,
    xn,
    sq_own,
    sq_all,
    f_own,
    f_all,
    f_col,
    wk,
    wo,
    own,
    onward,
    psend,
    precv,
    cand_n,
    gate_n,
    sweep_a,
    sweep_b,
    carry,
    ssend,
    sall,
    pout,
    osend,
    orecv,
    w_loc,
    w_snd,
    w_rcv,
    wo_sem,
    z_snd,
    z_rcv,
    k_snd,
    k_rcv,
    f_snd,
    q_snd,
    q_rcv,
    g_snd,
    g_rcv,
    p_snd,
    p_rcv,
    s_snd,
    s_rcv,
    o_snd,
    o_rcv,
):
    s, m = (lax.axis_index("seq"), lax.axis_index("mp"))
    n_chip = n_seq // CORES
    c, r = (s // CORES, s % CORES)
    mate = c * CORES + (1 - r)
    rows = tok_ref.shape[0]
    tokens = rows * n_seq
    k_own = wc_hbm.shape[0]
    width = raw.shape[2]
    q = r * n_chip + c

    def remote(src, dst, snd, rcv, **where):
        return pltpu.make_async_remote_copy(
            src_ref=src, dst_ref=dst, send_sem=snd, recv_sem=rcv, device_id=where, device_id_type=MESH
        )

    def barrier():
        sem = pltpu.get_barrier_semaphore()
        for o in range(1, n_seq):
            pl.semaphore_signal(sem, inc=1, device_id={"seq": (s + o) % n_seq}, device_id_type=MESH)
        for o in range(1, n_mp):
            pl.semaphore_signal(sem, inc=1, device_id={"mp": (m + o) % n_mp}, device_id_type=MESH)
        pl.semaphore_wait(sem, n_seq + n_mp - 2)

    def w_piece(hbm, core, chip):
        return hbm.at[:, pl.ds(pl.multiple_of((core * n_chip + chip) * LANES, LANES), LANES)]

    def w_place(i, chip, core):
        return wk.at[chip, pl.ds(pl.multiple_of(core * k_own, k_own), k_own), pl.ds(i * LANES, LANES)]

    local = [
        pltpu.make_async_copy(w_piece(hbm, r, chip), w_place(i, chip, r), w_loc.at[i, chip])
        for chip in range(n_chip)
        for i, hbm in enumerate((wc_hbm, wg_hbm))
    ]
    wo_copy = pltpu.make_async_copy(wo_hbm, wo, wo_sem)
    for copy in local:
        copy.start()
    barrier()

    part = rows // PIECES

    def piece(p):
        return pl.ds(p * part, part)

    def place(p, seq):
        return pl.ds(pl.multiple_of((p * n_seq + seq) * part, part), part)

    def z_copy(side, src, b, p, k):
        there = (m + 1) % n_mp if side == 0 else (m + n_mp - 1) % n_mp
        return remote(src, raw.at[b, piece(p)], z_snd.at[side, k, p], z_rcv.at[b, p], mp=there)

    def not_last(side):
        return m < n_mp - 1 if side == 0 else m > 0

    def plane_copy(src, b, p):
        seq = jnp.where(b == c, mate, b * CORES + r)
        return remote(src, xk.at[place(p, s)], k_snd.at[b, p], k_rcv.at[p, s], seq=seq)

    def send_own(p):
        mine = tok_ref.at[piece(p)]
        for side in range(2):

            @pl.when(not_last(side))
            def _():
                z_copy(side, mine, m, p, 0).start()

        plane_copy(mine, m, p).start()

        @pl.when(m == c)
        def _():
            xk[place(p, s), :] = tok_ref[piece(p), :]

    def pass_on(p, k):
        for side, sign in ((0, -1), (1, 1)):
            b = m + sign * k

            @pl.when((b >= 0) & (b <= n_mp - 1))
            def _():
                here = raw.at[b, piece(p)]
                z_copy(side, here, b, p, 0).wait_recv()

                @pl.when(not_last(side))
                def _():
                    z_copy(side, here, b, p, k).start()

                plane_copy(here, b, p).start()

                @pl.when(b == c)
                def _():
                    xk[place(p, s), :] = raw[b, piece(p), :]

    for p in range(min(2, PIECES)):
        send_own(p)

    across = lax.broadcasted_iota(jnp.int32, (rows, rows), 0) == lax.broadcasted_iota(
        jnp.int32, (rows, rows), 1
    )
    wide = tok_ref[...].astype(jnp.float32)
    squares = jnp.sum(wide * wide, axis=1, keepdims=True)
    squares = jnp.sum(jnp.where(across, squares, 0.0), axis=0, keepdims=True)
    sq_own[...] = jnp.broadcast_to(squares, sq_own.shape)
    sq_copies = []
    for o in range(1, n_mp):
        copy = remote(sq_own, sq_all.at[o], q_snd.at[o], q_rcv.at[o], mp=(m + o) % n_mp)
        copy.start()
        sq_copies.append(copy)

    w_out_copies = [
        remote(w_piece(hbm, 1 - r, chip), w_place(i, chip, r), w_snd.at[i, chip], w_rcv.at[i, chip], seq=mate)
        for chip in range(n_chip)
        for i, hbm in enumerate((wc_hbm, wg_hbm))
    ]
    for copy in w_out_copies:
        copy.start()
    wo_copy.start()
    gain = gain_ref[pl.ds(c, 1), :]
    bias = bg_ref[pl.ds(q, 1), :]
    rec_gate = rg_ref[pl.ds(q, 1), :]
    rec_cand = rc_ref[pl.ds(q, 1), :]
    tile = n_seq * part
    forward, f_copies = ([], [])

    def stage_a(turn):
        if turn + 2 < PIECES:
            send_own(turn + 2)
        for k in range(1, n_mp):
            p = turn - (k - 1)
            if 0 <= p < PIECES:
                pass_on(p, k)

    def factors():
        total = sq_own[...]
        for copy in sq_copies:
            copy.wait_recv()
        for o in range(1, n_mp):
            total = total + sq_all[o]
        f_own[...] = lax.rsqrt(total / (width * n_mp) + 1e-05)
        for o in range(1, n_seq):
            copy = remote(f_own, f_all.at[s], g_snd.at[o], g_rcv.at[s], seq=(s + o) % n_seq)
            copy.start()
            f_copies.append(copy)
        f_all[pl.ds(s, 1)] = f_own[...][None]

    def spread_factors():
        for o in range(1, n_seq):
            there = (s + o) % n_seq
            remote(f_own, f_all.at[there], g_snd.at[o], g_rcv.at[there], seq=there).wait_recv()
        for i in range(n_seq):
            row = f_all[i, 0:1, :]
            column = jnp.sum(jnp.where(across, row, 0.0), axis=1, keepdims=True)
            column = jnp.broadcast_to(column, (rows, LANES))
            for p in range(PIECES):
                f_col[(p * n_seq + i) * part : (p * n_seq + i + 1) * part, :] = column[
                    p * part : (p + 1) * part, :
                ]

    def arrived(p, seq):
        remote(tok_ref.at[piece(p)], xk.at[place(p, seq)], k_snd.at[0, p], k_rcv.at[p, seq], seq=mate).wait_recv()

    def stage_b(p):
        for o in range(1, n_chip):
            there = ((c + n_chip - o) % n_chip) * CORES + r
            arrived(p, there)
            copy = remote(
                xk.at[place(p, there)], xk.at[place(p, there)], f_snd.at[o, p], k_rcv.at[p, there], seq=mate
            )
            copy.start()
            forward.append(copy)

    def stage_c(p):
        for o in range(n_chip):
            arrived(p, ((c + n_chip - o) % n_chip) * CORES + (1 - r))

        @pl.loop(0, tile // GROUP)
        def _(i):
            at = pl.ds(pl.multiple_of(i * GROUP, GROUP), GROUP)
            of = pl.ds(pl.multiple_of(p * tile + i * GROUP, GROUP), GROUP)
            xn[at, :] = (xk[of, :].astype(jnp.float32) * f_col[of, 0:1] * gain).astype(jnp.bfloat16)

        def product(chip):
            return jnp.dot(xn[...], wk[chip], preferred_element_type=jnp.float32)

        at = pl.ds(p * tile, tile)
        first, second = ends(p)
        psend[1, at, :] = product(n_chip - 1 - c).astype(jnp.bfloat16)
        sums(1, p, first).start()
        psend[0, at, :] = product(first).astype(jnp.bfloat16)
        sums(0, p, first).start()
        onward[at, :] = product(second)
        own[at, :] = product(c)

    def ends(p):
        beside, above = (c + 1 - 2 * (c % 2), (c + n_chip // 2) % n_chip)
        return (beside, above) if p % 2 == 0 else (above, beside)

    def sums(slot, p, chip):
        at = pl.ds(p * tile, tile)
        return remote(
            psend.at[slot, at], precv.at[slot, at], p_snd.at[slot, p], p_rcv.at[slot, p], seq=chip * CORES + r
        )

    def stage_d(p):
        _, second = ends(p)
        sums(1, p, second).wait_recv()

        @pl.loop(0, tile // GROUP)
        def _(i):
            at = pl.ds(pl.multiple_of(p * tile + i * GROUP, GROUP), GROUP)
            psend[2, at, :] = (onward[at, :] + precv[1, at, :].astype(jnp.float32)).astype(jnp.bfloat16)

        sums(2, p, second).start()

    for turn in range(PIECES + n_mp + 1):
        stage_a(turn)
        if turn == 0:
            factors()
        if turn == 1:
            spread_factors()
            for copy in local:
                copy.wait()
            for copy in w_out_copies:
                copy.wait()
        if 0 <= turn - n_mp < PIECES:
            stage_c(turn - n_mp)
        if 0 <= turn - (n_mp - 1) < PIECES:
            stage_b(turn - (n_mp - 1))
        if 0 <= turn - (n_mp + 1) < PIECES:
            stage_d(turn - (n_mp + 1))

    def gather_piece(p):
        for slot in (0, 2):
            sums(slot, p, c).wait_recv()

        @pl.loop(0, tile // GROUP)
        def _(i):
            at = pl.ds(pl.multiple_of(p * tile + i * GROUP, GROUP), GROUP)
            value = own[at, :]
            for slot in (0, 2):
                value = value + precv[slot, at, :].astype(jnp.float32)
            cand_n[at, :] = value[:, :LANES]
            gate_n[at, :] = value[:, LANES:] + bias

    for newton_step in range(NEWTON):
        zero = jnp.zeros((n_seq, LANES), jnp.float32)
        entering = zero if newton_step == 0 else carry[...]
        held = (entering, zero + 1.0, zero)
        for p in range(PIECES):
            if newton_step == 0:
                gather_piece(p)

            def lap(i, held):
                previous, a, b = held
                j = p * part + i
                at = pl.ds(p * tile + i, n_seq, stride=part)
                value, slope = cell(previous, cand_n[at, :], gate_n[at, :], rec_gate, rec_cand, 0.0)
                offset = value - slope * previous
                if newton_step > 0:
                    previous = sweep_a[j] * entering + sweep_b[j]
                a, b = (slope * a, slope * b + offset)
                sweep_a[j] = a
                sweep_b[j] = b
                return (previous, a, b)

            held = lax.fori_loop(0, part, lap, held, unroll=8)
        _, a, b = held
        state = jnp.zeros((1, LANES), jnp.float32)
        for i in range(n_seq):
            carry[i : i + 1, :] = state
            state = a[i : i + 1, :] * state + b[i : i + 1, :]
    entering = carry[...]
    for p in range(PIECES):

        @pl.loop(0, part, unroll=8)
        def _(i):
            j = p * part + i
            cand_n[pl.ds(p * tile + i, n_seq, stride=part), :] = sweep_a[j] * entering + sweep_b[j]

    for i in range(n_seq):
        for p in range(PIECES):
            start = (p * n_seq + i) * part
            ssend[i, p * part : (p + 1) * part, :] = cand_n[start : start + part, :].astype(jnp.bfloat16)
    lane = pl.ds(pl.multiple_of(q * LANES, LANES), LANES)
    spread = []
    for o in range(1, n_seq):
        there = (s + o) % n_seq
        copy = remote(ssend.at[there], sall.at[:, lane], s_snd.at[o], s_rcv.at[o], seq=there)
        copy.start()
        spread.append(copy)
    sall[:, lane] = ssend[pl.ds(s, 1)].reshape(rows, LANES)
    wo_copy.wait()
    for copy in spread:
        copy.wait_recv()

    cols = out_ref.shape[1]
    half = rows // HALVES

    def hop(side, d, h):
        there = (m + 1) % n_mp if side == 0 else (m + n_mp - 1) % n_mp
        at = pl.ds(h * half, half)
        return remote(
            osend.at[d, at], orecv.at[side, d, at], o_snd.at[d, h], o_rcv.at[side, d, h], mp=there
        )

    def project(d):
        lanes = pl.ds(pl.multiple_of(d * cols, cols), cols)
        pout[...] = jnp.dot(sall[...], wo[:, lanes], preferred_element_type=jnp.float32)

    for k in range(n_mp - 1, 0, -1):
        for side, sign in ((0, 1), (1, -1)):
            d = m + sign * k
            inside = (d <= n_mp - 1) if side == 0 else (d >= 0)
            first = (m == 0) if side == 0 else (m == n_mp - 1)

            @pl.when(inside)
            def _():
                project(d)
                for h in range(HALVES):
                    at = pl.ds(h * half, half)

                    @pl.when(first)
                    def _():
                        osend[d, at, :] = pout[at, :].astype(jnp.bfloat16)

                    @pl.when(jnp.logical_not(first))
                    def _():
                        hop(side, d, h).wait_recv()
                        osend[d, at, :] = (pout[at, :] + orecv[side, d, at, :].astype(jnp.float32)).astype(
                            jnp.bfloat16
                        )

                    hop(side, d, h).start()

    project(m)
    for side in range(2):

        @pl.when(m > 0 if side == 0 else m < n_mp - 1)
        def _():
            for h in range(HALVES):
                at = pl.ds(h * half, half)
                hop(side, m, h).wait_recv()
                pout[at, :] = pout[at, :] + orecv[side, m, at, :].astype(jnp.float32)

    out_ref[...] = pout[...].astype(jnp.bfloat16)

    for p in range(PIECES):
        for k in range(n_mp):
            for side, sign in ((0, -1), (1, 1)):
                b = m + sign * k

                @pl.when(not_last(side) & (b >= 0) & (b <= n_mp - 1))
                def _():
                    z_copy(side, tok_ref.at[piece(p)], b, p, k).wait_send()

            plane_copy(tok_ref.at[piece(p)], k, p).wait_send()
        for slot in range(3):
            sums(slot, p, c).wait_send()

    for copy in sq_copies + f_copies + forward + spread:
        copy.wait_send()
    for d in range(n_mp):

        @pl.when(d != m)
        def _():
            for h in range(HALVES):
                hop(0, d, h).wait_send()


def fused(n_seq, n_mp, tokens, norm_gain, w_cand, w_gate, rec_gate, rec_cand, bias_gate, w_out):
    rows, width = tokens.shape
    k_own, channels = w_cand.shape
    n_chip = n_seq // CORES
    length = rows * n_seq
    bf16, f32 = (jnp.bfloat16, jnp.float32)
    vmem, dma = (pltpu.VMEM, pltpu.SemaphoreType.DMA)
    whole = pl.BlockSpec(memory_space=pltpu.VMEM)
    far = pl.BlockSpec(memory_space=pl.ANY)
    per_channel = [part.reshape(n_seq, LANES) for part in (rec_gate, rec_cand, bias_gate)]
    return pl.pallas_call(
        functools.partial(fused_kernel, n_seq, n_mp),
        out_shape=jax.ShapeDtypeStruct((rows, width), bf16),
        in_specs=[whole, whole, far, far, whole, whole, whole, far],
        out_specs=whole,
        scratch_shapes=[
            vmem((n_mp, rows, width), bf16),
            vmem((length, width), bf16),
            vmem((length // PIECES, width), bf16),
            vmem((n_seq, LANES), f32),
            vmem((n_mp, n_seq, LANES), f32),
            vmem((n_seq, LANES), f32),
            vmem((n_seq, n_seq, LANES), f32),
            vmem((length, LANES), f32),
            vmem((n_chip, k_own * CORES, 2 * LANES), bf16),
            vmem(w_out.shape, bf16),
            vmem((length, 2 * LANES), f32),
            vmem((length, 2 * LANES), f32),
            vmem((n_chip - 1, length, 2 * LANES), bf16),
            vmem((n_chip - 1, length, 2 * LANES), bf16),
            vmem((length, LANES), f32),
            vmem((length, LANES), f32),
            vmem((rows, n_seq, LANES), f32),
            vmem((rows, n_seq, LANES), f32),
            vmem((n_seq, LANES), f32),
            vmem((n_seq, rows, LANES), bf16),
            vmem((rows, channels), bf16),
            vmem((rows, width), f32),
            vmem((n_mp, rows, width), bf16),
            vmem((2, n_mp, rows, width), bf16),
            dma((2, n_chip)),
            dma((2, n_chip)),
            dma((2, n_chip)),
            dma,
            dma((2, n_mp, PIECES)),
            dma((n_mp, PIECES)),
            dma((n_mp, PIECES)),
            dma((PIECES, n_seq)),
            dma((n_chip, PIECES)),
            dma((n_mp,)),
            dma((n_mp,)),
            dma((n_seq,)),
            dma((n_seq,)),
            dma((n_chip, PIECES)),
            dma((n_chip, PIECES)),
            dma((n_seq,)),
            dma((n_seq,)),
            dma((n_mp, HALVES)),
            dma((2, n_mp, HALVES)),
        ],
        compiler_params=pltpu.CompilerParams(collective_id=0, has_side_effects=True),
    )(tokens, norm_gain.reshape(n_mp, -1), w_cand, w_gate, *per_channel, w_out)


def layer(n_seq, n_mp, *args):
    tokens, w_cand = (args[0], args[2])
    fits = (
        n_seq == SUBLANES
        and n_seq == 4 * CORES
        and n_seq // CORES == n_mp
        and w_cand.shape[1] == n_seq * LANES
        and tokens.shape[0] == LANES
        and tokens.shape[1] % LANES == 0
    )
    return fused(n_seq, n_mp, *args) if fits else per_device(*args)


def solution(mesh):
    placed = (
        P("seq", "mp"),
        P(),
        P("seq", "mp"),
        P("seq", "mp"),
        P("mp"),
        P("mp"),
        P("mp"),
        P("mp", None),
    )
    return jax.shard_map(
        functools.partial(layer, mesh.shape["seq"], mesh.shape["mp"]), mesh=mesh, in_specs=placed, out_specs=P("seq", "mp"), check_vma=False
    )
```

profile of v0, /device:TPU:0, one launch (start us, length us, event | category | flops | bytes accessed | tf_op | source)
XLA Modules:
  0.0 85.5 jit_solution(6455330265855773272)
XLA Ops:
  0.0 1.3 %reshape.12.gain_ref = f32[4,1024]{1,0:T(4,128)} reshape(f32[4096]{0:T(1024)} %param.9) | data formatting | bytes 32768 | tf_op jit(solution)/shard_map/reshape | solution.py:570
  1.3 82.5 %shard_map.82 = bf16[128,1024]{1,0:T(8,128)(2,1)} custom-call(bf16[128,1024]{1,0:T(8,128)(2,1)} %tok_ref.1, f32[4,1024]{1,0:T(4,128)} %reshape.12.gain_ref, bf16[512,1024]{1,0:T(8,128)(2,1)} %wc_hbm.1, bf16[512,1024]{1,0:T(8,128)(2,1)} %wg_hbm.1, f32[8,128]{1,0:T(8,128)} %bitcast.3, f32[8,128]{1,0:T(8,128)} %bitcast.4, f32[8,128]{1,0:T(8,128)} %bitcast.5, ...), custom_call_target="tpu_custom_call" | custom-call | tf_op jit(solution)/shard_map/pallas_call | solution.py:519
  83.8 1.7 %copy.10 = bf16[128,1024]{1,0:T(8,128)(2,1)} copy(bf16[128,1024]{1,0:T(8,128)(2,1)} %shard_map.82) | data formatting | bytes 524288
where the time goes:
time: 85.7 us; the launch traced here: 85.5 us
  Pallas kernels  82.5 us (96%)
  local copies, waits for them, and re-layouts  3 us (4%)
    pallas_call x1, Pallas kernels, fused(): pl.pallas_call(functools.partial(fused_kernel, n_seq, n_mp), out_shape=ja...  82.5 us

commit v1 on v0

v1 whole, which is shorter than its diff:
```python
import functools

import jax
import jax.numpy as jnp
from jax import lax
from jax.experimental import pallas as pl
from jax.experimental.pallas import tpu as pltpu
from jax.sharding import PartitionSpec as P

NEWTON = 3


def prefix(value, axis, join, neutral):
    count, mine = (lax.axis_size(axis), lax.axis_index(axis))
    pieces = jax.tree.map(lambda part: lax.all_gather(part, axis), value)
    subtotal = jax.tree.map(
        lambda part, zero: jnp.full_like(part, 0) + jnp.asarray(zero, part.dtype), value, neutral
    )

    def lap(position, subtotal):
        longer = join(subtotal, jax.tree.map(lambda part: part[position], pieces))
        return jax.tree.map(lambda new, old: jnp.where(position < mine, new, old), longer, subtotal)

    return lax.fori_loop(0, count - 1, lap, subtotal)


def compose(earlier, later):
    return (later[0] * earlier[0], later[0] * earlier[1] + later[1])


def cell(previous, cand_pre, gate_pre, rec_gate, rec_cand, bias_gate):
    gate = jax.nn.sigmoid(gate_pre + rec_gate * previous + bias_gate)
    cand = jnp.tanh(cand_pre + rec_cand * previous)
    value = gate * previous + (1.0 - gate) * cand
    slope = (
        gate
        + gate * (1.0 - gate) * rec_gate * (previous - cand)
        + (1.0 - gate) * (1.0 - cand * cand) * rec_cand
    )
    return (value, slope)


def per_device(tokens, norm_gain, w_cand, w_gate, rec_gate, rec_cand, bias_gate, w_out):
    tok_rows = tokens.shape[0]
    channels = w_cand.shape[1]
    whole = lax.all_gather(tokens, "mp", axis=1, tiled=True)
    wide = whole.astype(jnp.float32)
    factor = lax.rsqrt(jnp.mean(wide * wide, axis=1, keepdims=True) + 1e-05)
    normed = (wide * factor * norm_gain).astype(jnp.bfloat16)
    cand_pre = jnp.dot(
        normed,
        lax.all_gather(w_cand, "seq", axis=0, tiled=True),
        preferred_element_type=jnp.float32,
    )
    gate_pre = jnp.dot(
        normed,
        lax.all_gather(w_gate, "seq", axis=0, tiled=True),
        preferred_element_type=jnp.float32,
    )
    state = jnp.zeros((tok_rows, channels), jnp.float32)
    carried = jnp.zeros((channels,), jnp.float32)
    ones_row = jnp.ones((channels,), jnp.float32)
    for newton_step in range(NEWTON):
        previous = jnp.concatenate([carried[None, :], state[:-1]], axis=0)
        value, slope = cell(previous, cand_pre, gate_pre, rec_gate, rec_cand, bias_gate)
        offset = value - slope * previous
        sweep_a, sweep_b = lax.associative_scan(compose, (slope, offset), axis=0)
        entering = prefix((sweep_a[-1], sweep_b[-1]), "seq", compose, (ones_row, carried * 0.0))
        carried = entering[1]
        state = sweep_a * carried + sweep_b
    state_b = state.astype(jnp.bfloat16)
    partial_sums = jnp.dot(state_b, w_out, preferred_element_type=jnp.float32)
    summed = lax.psum_scatter(partial_sums, "mp", scatter_dimension=1, tiled=True)
    return summed.astype(jnp.bfloat16)


def linear(first, previous, cand_pre, half_pre, half_gate, rec_gate, rec_cand):
    if first:
        gate = 0.5 * jnp.tanh(half_pre) + 0.5
        cand = jnp.tanh(cand_pre)
        apart = -cand
    else:
        gate = 0.5 * jnp.tanh(half_pre + half_gate * previous) + 0.5
        cand = jnp.tanh(cand_pre + rec_cand * previous)
        apart = previous - cand
    other = 1.0 - gate
    moved = gate * apart
    slope = gate + other * (rec_gate * moved + rec_cand * (1.0 - cand * cand))
    offset = cand + moved
    return slope, offset if first else offset - slope * previous


CORES = 2
SUBLANES = 8
LANES = 128
SIZES = (16,) * 8
PIECES = len(SIZES)
STARTS = tuple(sum(SIZES[:i]) for i in range(PIECES))
HALVES = 2
LAG = 2
LOOK = 2
WO_TURN = 8
UNROLL = 4
OWN = 1
BL = 1
CL = 2
ORDER = "cbd"
GROUP = 16
MESH = pl.DeviceIdType.MESH


def fused_kernel(
    n_seq,
    n_mp,
    tok_hbm,
    gain_ref,
    wc_hbm,
    wg_hbm,
    rg_ref,
    rc_ref,
    bg_ref,
    wo_hbm,
    out_ref,
    tok_ref,
    raw,
    xk,
    xn,
    sq_own,
    sq_all,
    f_own,
    f_all,
    f_col,
    wk,
    wo,
    own,
    onward,
    psend,
    precv,
    cand_n,
    gate_n,
    sweep_a,
    sweep_b,
    carry,
    ssend,
    sall,
    pout,
    osend,
    orecv,
    w_loc,
    w_snd,
    w_rcv,
    wo_sem,
    tok_sem,
    z_snd,
    z_rcv,
    k_snd,
    k_rcv,
    f_snd,
    q_snd,
    q_rcv,
    g_snd,
    g_rcv,
    p_snd,
    p_rcv,
    s_snd,
    s_rcv,
    o_snd,
    o_rcv,
):
    s, m = (lax.axis_index("seq"), lax.axis_index("mp"))
    n_chip = n_seq // CORES
    c, r = (s // CORES, s % CORES)
    mate = c * CORES + (1 - r)
    rows = tok_ref.shape[0]
    tokens = rows * n_seq
    k_own = wc_hbm.shape[0]
    width = raw.shape[2]
    q = r * n_chip + c

    def remote(src, dst, snd, rcv, **where):
        return pltpu.make_async_remote_copy(
            src_ref=src, dst_ref=dst, send_sem=snd, recv_sem=rcv, device_id=where, device_id_type=MESH
        )

    def greet():
        sem = pltpu.get_barrier_semaphore()
        for o in range(1, n_seq):
            pl.semaphore_signal(sem, inc=1, device_id={"seq": (s + o) % n_seq}, device_id_type=MESH)
        for o in range(1, n_mp):
            pl.semaphore_signal(sem, inc=1, device_id={"mp": (m + o) % n_mp}, device_id_type=MESH)

    def w_piece(hbm, core, chip):
        return hbm.at[:, pl.ds(pl.multiple_of((core * n_chip + chip) * LANES, LANES), LANES)]

    def w_place(i, chip, core):
        return wk.at[chip, pl.ds(pl.multiple_of(core * k_own, k_own), k_own), pl.ds(i * LANES, LANES)]

    local = [
        pltpu.make_async_copy(w_piece(hbm, r, chip), w_place(i, chip, r), w_loc)
        for chip in range(n_chip)
        for i, hbm in enumerate((wc_hbm, wg_hbm))
    ]
    wo_copy = pltpu.make_async_copy(wo_hbm, wo, wo_sem)
    greet()
    tok_copy = pltpu.make_async_copy(tok_hbm, tok_ref, tok_sem)
    tok_copy.start()
    for copy in local:
        copy.start()
    tok_copy.wait()
    across = lax.broadcasted_iota(jnp.int32, (rows, rows), 0) == lax.broadcasted_iota(
        jnp.int32, (rows, rows), 1
    )
    wide = tok_ref[...].astype(jnp.float32)
    squares = jnp.sum(wide * wide, axis=1, keepdims=True)
    squares = jnp.sum(jnp.where(across, squares, 0.0), axis=0, keepdims=True)
    sq_own[...] = jnp.broadcast_to(squares, sq_own.shape)
    pl.semaphore_wait(pltpu.get_barrier_semaphore(), n_seq + n_mp - 2)

    def piece(p):
        return pl.ds(STARTS[p], SIZES[p])

    def place(p, seq):
        return pl.ds(pl.multiple_of(STARTS[p] * n_seq + seq * SIZES[p], SUBLANES * 2), SIZES[p])

    def block(p):
        return pl.ds(STARTS[p] * n_seq, SIZES[p] * n_seq)

    def z_copy(src, b, p, d):
        return remote(src, raw.at[b, piece(p)], z_snd, z_rcv.at[b, p], mp=d)

    def relayed(b, d):
        return ((b == 1) & (d == 3)) | ((b == 2) & (d == 0))

    def plane_copy(src, b, p):
        seq = jnp.where(b == c, mate, b * CORES + r)
        lane_in = jnp.where(b == c, 1, 0)
        return remote(src, xk.at[place(p, s)], k_snd, k_rcv.at[lane_in, p], seq=seq)

    def z_send(p):
        for d in range(n_mp - 1, 0, -1):

            @pl.when((d > m) & jnp.logical_not(relayed(m, d)))
            def _():
                z_copy(tok_ref.at[piece(p)], m, p, d).start()

        for d in range(n_mp - 1):

            @pl.when((d < m) & jnp.logical_not(relayed(m, d)))
            def _():
                z_copy(tok_ref.at[piece(p)], m, p, d).start()

    def send_own(p):
        plane_copy(tok_ref.at[piece(p)], m, p).start()

        @pl.when(m == c)
        def _():
            xk[place(p, s), :] = tok_ref[piece(p), :]

    def pass_on(p, k):
        for sign in (-1, 1):
            b = m + sign * k

            @pl.when((b >= 0) & (b <= n_mp - 1))
            def _():
                here = raw.at[b, piece(p)]
                z_copy(here, b, p, m).wait_recv()
                if k == 1:
                    far = n_mp - 1 if sign < 0 else 0

                    @pl.when(m == (n_mp - 2 if sign < 0 else 1))
                    def _():
                        z_copy(here, b, p, far).start()

                plane_copy(here, b, p).start()

                @pl.when(b == c)
                def _():
                    xk[place(p, s), :] = raw[b, piece(p), :]

    for o in range(1, n_mp):
        copy = remote(sq_own, sq_all.at[o], q_snd, q_rcv, mp=(m + o) % n_mp)
        copy.start()
    for p in range(LOOK):
        z_send(p)
    for p in range(OWN):
        send_own(p)

    w_out_copies = [
        remote(w_piece(hbm, 1 - r, chip), w_place(i, chip, r), w_snd, w_rcv, seq=mate)
        for chip in range(n_chip)
        for i, hbm in enumerate((wc_hbm, wg_hbm))
    ]
    for copy in w_out_copies:
        copy.start()
    wide_rows = width // LANES
    gain = jnp.concatenate([gain_ref[pl.ds(c * wide_rows + i, 1), :] for i in range(wide_rows)], axis=1)
    bias = bg_ref[pl.ds(q, 1), :]
    half_gate = rg_ref[pl.ds(q, 1), :] * 0.5
    rec_gate = rg_ref[pl.ds(q, 1), :]
    rec_cand = rc_ref[pl.ds(q, 1), :]

    def stage_a(p):
        if p + LOOK < PIECES:
            z_send(p + LOOK)
        if p + OWN < PIECES:
            send_own(p + OWN)
        for k in range(1, n_mp):
            pass_on(p, k)
            if p == 0 and k == 1:
                factors()

    def factors():
        total = sq_own[...]
        others = sq_all.at[pl.ds(1, n_mp - 1)]
        remote(others, others, q_snd, q_rcv, mp=m).wait_recv()
        for o in range(1, n_mp):
            total = total + sq_all[o]
        f_own[...] = lax.rsqrt(total / (width * n_mp) + 1e-05)
        for o in range(1, n_seq):
            copy = remote(f_own, f_all.at[s], g_snd, g_rcv, seq=(s + o) % n_seq)
            copy.start()
        f_all[pl.ds(s, 1)] = f_own[...][None]

    def spread_factors():
        others = f_all.at[pl.ds(1, n_seq - 1)]
        remote(others, others, g_snd, g_rcv, seq=s).wait_recv()
        for i in range(n_seq):
            row = f_all[i, 0:1, :]
            column = jnp.sum(jnp.where(across, row, 0.0), axis=1, keepdims=True)
            column = jnp.broadcast_to(column, (rows, LANES))
            for start, size in zip(STARTS, SIZES):
                f_col[start * n_seq + i * size : start * n_seq + (i + 1) * size, :] = column[start : start + size, :]

    def arrived(p, lane_in):
        of = xk.at[pl.ds(0, (n_chip - 1 + lane_in) * SIZES[p])]
        remote(of, of, k_snd, k_rcv.at[lane_in, p], seq=s).wait_recv()

    def stage_b(p):
        arrived(p, 0)
        for o in range(1, n_chip):
            there = ((c + n_chip - o) % n_chip) * CORES + r
            copy = remote(
                xk.at[place(p, there)], xk.at[place(p, there)], f_snd, k_rcv.at[1, p], seq=mate
            )
            copy.start()

    def stage_c(p):
        arrived(p, 1)

        tile = SIZES[p] * n_seq

        @pl.loop(0, tile // GROUP, unroll=UNROLL)
        def _(i):
            at = pl.ds(pl.multiple_of(i * GROUP, GROUP), GROUP)
            of = pl.ds(pl.multiple_of(STARTS[p] * n_seq + i * GROUP, GROUP), GROUP)
            xn[at, :] = (xk[of, :].astype(jnp.float32) * f_col[of, 0:1] * gain).astype(jnp.bfloat16)

        def product(chip):
            return jnp.dot(xn[:tile, :], wk[chip], preferred_element_type=jnp.float32)

        at = block(p)
        first, second = ends(p)
        psend[1, at, :] = product(n_chip - 1 - c).astype(jnp.bfloat16)
        sums(1, p, first).start()
        psend[0, at, :] = product(first).astype(jnp.bfloat16)
        sums(0, p, first).start()
        onward[at, :] = product(second)
        own[at, :] = product(c)

    def ends(p):
        beside, above = (c + 1 - 2 * (c % 2), (c + n_chip // 2) % n_chip)
        return (beside, above) if p % 2 == 0 else (above, beside)

    def sums(slot, p, chip):
        at = block(p)
        return remote(
            psend.at[slot, at], precv.at[slot, at], p_snd, p_rcv.at[int(slot != 1), p], seq=chip * CORES + r
        )

    def stage_d(p):
        _, second = ends(p)
        sums(1, p, second).wait_recv()

        @pl.loop(0, SIZES[p] * n_seq // GROUP)
        def _(i):
            at = pl.ds(pl.multiple_of(STARTS[p] * n_seq + i * GROUP, GROUP), GROUP)
            psend[2, at, :] = (onward[at, :] + precv[1, at, :].astype(jnp.float32)).astype(jnp.bfloat16)

        sums(2, p, second).start()

    for turn in range(PIECES + CL + LAG):
        if turn < PIECES:
            stage_a(turn)
        if turn == CL - 1:
            spread_factors()
            part = wk.at[pl.ds(0, n_chip // 2)]
            pltpu.make_async_copy(part, part, w_loc).wait()
            remote(part, part, w_snd, w_rcv, seq=s).wait_recv()
        if turn == WO_TURN:
            wo_copy.start()
        for what in ORDER:
            if what == "c" and 0 <= turn - CL < PIECES:
                stage_c(turn - CL)
            if what == "b" and 0 <= turn - BL < PIECES:
                stage_b(turn - BL)
            if what == "d" and 0 <= turn - CL - LAG < PIECES:
                stage_d(turn - CL - LAG)

    def gather_piece(p):
        both = precv.at[pl.ds(0, 2), block(p)]
        remote(both, both, p_snd, p_rcv.at[1, p], seq=s).wait_recv()

        @pl.loop(0, SIZES[p] * n_seq // GROUP)
        def _(i):
            at = pl.ds(pl.multiple_of(STARTS[p] * n_seq + i * GROUP, GROUP), GROUP)
            value = own[at, :]
            for slot in (0, 2):
                value = value + precv[slot, at, :].astype(jnp.float32)
            cand_n[at, :] = value[:, :LANES]
            gate_n[at, :] = (value[:, LANES:] + bias) * 0.5

    for newton_step in range(NEWTON):
        zero = jnp.zeros((n_seq, LANES), jnp.float32)
        entering = zero if newton_step == 0 else carry[...]
        held = (entering, zero + 1.0, zero)
        for p in range(PIECES):
            if newton_step == 0:
                gather_piece(p)

            def lap(i, held):
                previous, a, b = held
                j = STARTS[p] + i
                at = pl.ds(STARTS[p] * n_seq + i, n_seq, stride=SIZES[p])
                slope, offset = linear(newton_step == 0, previous, cand_n[at, :], gate_n[at, :], half_gate, rec_gate, rec_cand)
                if newton_step > 0:
                    previous = sweep_a[j] * entering + sweep_b[j]
                a, b = (slope * a, slope * b + offset)
                sweep_a[j] = a
                sweep_b[j] = b
                return (previous, a, b)

            held = lax.fori_loop(0, SIZES[p], lap, held, unroll=8)
        _, a, b = held
        state = jnp.zeros((1, LANES), jnp.float32)
        for i in range(n_seq):
            carry[i : i + 1, :] = state
            state = a[i : i + 1, :] * state + b[i : i + 1, :]
    entering = carry[...]
    for p in range(PIECES):

        @pl.loop(0, SIZES[p], unroll=8)
        def _(i):
            j = STARTS[p] + i
            cand_n[pl.ds(STARTS[p] * n_seq + i, n_seq, stride=SIZES[p]), :] = sweep_a[j] * entering + sweep_b[j]

    for i in range(n_seq):
        for p in range(PIECES):
            start, size = STARTS[p] * n_seq + i * SIZES[p], SIZES[p]
            ssend[i, piece(p), :] = cand_n[start : start + size, :].astype(jnp.bfloat16)
    lane = pl.ds(pl.multiple_of(q * LANES, LANES), LANES)
    for o in range(1, n_seq):
        there = (s + o) % n_seq
        copy = remote(ssend.at[there], sall.at[:, lane], s_snd, s_rcv, seq=there)
        copy.start()
    sall[:, lane] = ssend[pl.ds(s, 1)].reshape(rows, LANES)
    def sent(ref, sem):
        remote(ref, ref, sem, s_rcv, seq=s).wait_send()

    sent(wk.at[pl.ds(0, n_chip // 2)], w_snd)
    sent(raw.at[pl.ds(0, n_mp - 1)], z_snd)
    sent(raw, k_snd)
    sent(raw.at[pl.ds(0, n_chip - 1)], f_snd)
    sent(sq_all.at[pl.ds(1, n_mp - 1)], q_snd)
    sent(f_all.at[pl.ds(1, n_seq - 1)], g_snd)
    sent(psend, p_snd)
    wo_copy.wait()
    others = ssend.at[pl.ds(1, n_seq - 1)]
    remote(others, others, s_snd, s_rcv, seq=s).wait_recv()

    cols = out_ref.shape[1]
    half = rows // HALVES

    def hop(side, d, h):
        there = (m + 1) % n_mp if side == 0 else (m + n_mp - 1) % n_mp
        at = pl.ds(h * half, half)
        return remote(
            osend.at[d, at], orecv.at[side, d, at], o_snd, o_rcv.at[side, d, h], mp=there
        )

    def project(d):
        lanes = pl.ds(pl.multiple_of(d * cols, cols), cols)
        pout[...] = jnp.dot(sall[...], wo[:, lanes], preferred_element_type=jnp.float32)

    def send_sum(side, k, when):
        d = m + k if side == 0 else m - k
        inside = (d <= n_mp - 1) if side == 0 else (d >= 0)
        first = (m == 0) if side == 0 else (m == n_mp - 1)

        @pl.when(inside & when)
        def _():
            project(d)
            for h in range(HALVES):
                at = pl.ds(h * half, half)

                @pl.when(first)
                def _():
                    osend[d, at, :] = pout[at, :].astype(jnp.bfloat16)

                @pl.when(jnp.logical_not(first))
                def _():
                    hop(side, d, h).wait_recv()
                    osend[d, at, :] = (pout[at, :] + orecv[side, d, at, :].astype(jnp.float32)).astype(
                        jnp.bfloat16
                    )

                hop(side, d, h).start()

    for k in range(n_mp - 1, 1, -1):
        for side in range(2):
            send_sum(side, k, True)
    low = m < n_mp // 2
    send_sum(1, 1, low)
    send_sum(0, 1, True)
    send_sum(1, 1, jnp.logical_not(low))

    project(m)
    for side in range(2):

        @pl.when(m > 0 if side == 0 else m < n_mp - 1)
        def _():
            for h in range(HALVES):
                at = pl.ds(h * half, half)
                hop(side, m, h).wait_recv()
                pout[at, :] = pout[at, :] + orecv[side, m, at, :].astype(jnp.float32)

    out_ref[...] = pout[...].astype(jnp.bfloat16)

    sent(ssend.at[pl.ds(1, n_seq - 1)], s_snd)
    sent(osend.at[pl.ds(1, n_mp - 1)], o_snd)


def fused(n_seq, n_mp, tokens, norm_gain, w_cand, w_gate, rec_gate, rec_cand, bias_gate, w_out):
    rows, width = tokens.shape
    k_own, channels = w_cand.shape
    n_chip = n_seq // CORES
    length = rows * n_seq
    bf16, f32 = (jnp.bfloat16, jnp.float32)
    vmem, dma = (pltpu.VMEM, pltpu.SemaphoreType.DMA)
    whole = pl.BlockSpec(memory_space=pltpu.VMEM)
    far = pl.BlockSpec(memory_space=pl.ANY)
    per_channel = [part.reshape(n_seq, LANES) for part in (rec_gate, rec_cand, bias_gate)]
    return pl.pallas_call(
        functools.partial(fused_kernel, n_seq, n_mp),
        out_shape=pltpu.VMEM((rows, width), bf16),
        in_specs=[far, whole, far, far, whole, whole, whole, far],
        out_specs=whole,
        scratch_shapes=[
            vmem((rows, width), bf16),
            vmem((n_mp, rows, width), bf16),
            vmem((length, width), bf16),
            vmem((length * max(SIZES) // sum(SIZES), width), bf16),
            vmem((n_seq, LANES), f32),
            vmem((n_mp, n_seq, LANES), f32),
            vmem((n_seq, LANES), f32),
            vmem((n_seq, n_seq, LANES), f32),
            vmem((length, LANES), f32),
            vmem((n_chip, k_own * CORES, 2 * LANES), bf16),
            vmem(w_out.shape, bf16),
            vmem((length, 2 * LANES), f32),
            vmem((length, 2 * LANES), f32),
            vmem((n_chip - 1, length, 2 * LANES), bf16),
            vmem((n_chip - 1, length, 2 * LANES), bf16),
            vmem((length, LANES), f32),
            vmem((length, LANES), f32),
            vmem((rows, n_seq, LANES), f32),
            vmem((rows, n_seq, LANES), f32),
            vmem((n_seq, LANES), f32),
            vmem((n_seq, rows, LANES), bf16),
            vmem((rows, channels), bf16),
            vmem((rows, width), f32),
            vmem((n_mp, rows, width), bf16),
            vmem((2, n_mp, rows, width), bf16),
            dma,
            dma,
            dma,
            dma,
            dma,
            dma,
            dma((n_mp, PIECES)),
            dma,
            dma((2, PIECES)),
            dma,
            dma,
            dma,
            dma,
            dma,
            dma,
            dma((2, PIECES)),
            dma,
            dma,
            dma,
            dma((2, n_mp, HALVES)),
        ],
        compiler_params=pltpu.CompilerParams(collective_id=0, has_side_effects=True),
    )(tokens, norm_gain.reshape(-1, LANES), w_cand, w_gate, *per_channel, w_out)


def layer(n_seq, n_mp, *args):
    tokens, w_cand = (args[0], args[2])
    fits = (
        n_seq == SUBLANES
        and n_seq == 4 * CORES
        and n_seq // CORES == n_mp
        and w_cand.shape[1] == n_seq * LANES
        and tokens.shape[0] == LANES
        and tokens.shape[1] % LANES == 0
    )
    return fused(n_seq, n_mp, *args) if fits else per_device(*args)


def solution(mesh):
    placed = (
        P("seq", "mp"),
        P(),
        P("seq", "mp"),
        P("seq", "mp"),
        P("mp"),
        P("mp"),
        P("mp"),
        P("mp", None),
    )
    return jax.shard_map(
        functools.partial(layer, mesh.shape["seq"], mesh.shape["mp"]), mesh=mesh, in_specs=placed, out_specs=P("seq", "mp"), check_vma=False
    )
```

time: 85.7 us -> 74 us (0.86)
  Pallas kernels: 82.5 us -> 73.1 us
  local copies, waits for them, and re-layouts: 3 us -> 0.71 us
    pallas_call x1, Pallas kernels: 82.5 us -> 73.1 us  [fused(): pl.pallas_call(functools.partial(fused_kernel, n_seq, n_mp), out_shape=pl...]
    reshape x1 -> x0, local copies, waits for them, and re-layouts: 1.33 us -> none  [fused(): norm_gain.reshape(n_mp, -1)]
    unnamed x1, local copies, waits for them, and re-layouts: 1.67 us -> 0.71 us
where the time goes in v1:
time: 74 us; the launch traced here: 73.8 us
  Pallas kernels  73.1 us (99%)
    pallas_call x1, Pallas kernels, fused(): pl.pallas_call(functools.partial(fused_kernel, n_seq, n_mp), out_shape=pl...  73.1 us

profile of v1, /device:TPU:0, one launch (start us, length us, event | category | flops | bytes accessed | tf_op | source)
XLA Modules:
  0.0 73.8 jit_solution(12010547296401839212)
XLA Ops:
  0.0 73.1 %shard_map.82 = bf16[128,1024]{1,0:T(8,128)(2,1)S(1)} custom-call(bf16[128,1024]{1,0:T(8,128)(2,1)} %tok_hbm.1, f32[32,128]{1,0:T(8,128)} %bitcast.4, bf16[512,1024]{1,0:T(8,128)(2,1)} %wc_hbm.1, bf16[512,1024]{1,0:T(8,128)(2,1)} %wg_hbm.1, f32[8,128]{1,0:T(8,128)} %bitcast.5, f32[8,128]{1,0:T(8,128)} %bitcast.6, f32[8,128]{1,0:T(8,128)} %bitcast.7, ...), custom_call_target="tpu_custom_call" | custom-call | tf_op jit(solution)/shard_map/pallas_call | solution.py:552
  73.1 0.7 copy.10

commit v2 on v1

--- a/solution.py
+++ b/solution.py
@@ -93,18 +93,21 @@
 CORES = 2
 SUBLANES = 8
 LANES = 128
-SIZES = (16,) * 8
+SIZES = (16, 16, 32, 32, 32)
 PIECES = len(SIZES)
 STARTS = tuple(sum(SIZES[:i]) for i in range(PIECES))
 HALVES = 2
+RELAY = 1
+NEAR = 1
+FACTORS_AT = (0, 2)
 LAG = 2
 LOOK = 2
-WO_TURN = 8
+WO_TURN = 5
 UNROLL = 4
 OWN = 1
 BL = 1
 CL = 2
-ORDER = "cbd"
+ORDER = "acbd"
 GROUP = 16
 MESH = pl.DeviceIdType.MESH
 
@@ -113,15 +116,19 @@
     n_seq,
     n_mp,
     tok_hbm,
-    gain_ref,
+    gain_hbm,
     wc_hbm,
     wg_hbm,
+    rg_hbm,
+    rc_hbm,
+    bg_hbm,
+    wo_hbm,
+    out_ref,
+    tok_ref,
+    gain_ref,
     rg_ref,
     rc_ref,
     bg_ref,
-    wo_hbm,
-    out_ref,
-    tok_ref,
     raw,
     xk,
     xn,
@@ -151,6 +158,7 @@
     w_rcv,
     wo_sem,
     tok_sem,
+    small_sem,
     z_snd,
     z_rcv,
     k_snd,
@@ -206,7 +214,83 @@
     tok_copy.start()
     for copy in local:
         copy.start()
+    small = [
+        pltpu.make_async_copy(src, dst, small_sem.at[i])
+        for i, (src, dst) in enumerate(
+            ((gain_hbm, gain_ref), (rg_hbm, rg_ref), (rc_hbm, rc_ref), (bg_hbm, bg_ref))
+        )
+    ]
+    for copy in small:
+        copy.start()
+    pl.semaphore_wait(pltpu.get_barrier_semaphore(), n_seq + n_mp - 2)
     tok_copy.wait()
+
+    def piece(p):
+        return pl.ds(STARTS[p], SIZES[p])
+
+    def place(p, seq):
+        return pl.ds(pl.multiple_of(STARTS[p] * n_seq + seq * SIZES[p], SUBLANES * 2), SIZES[p])
+
+    def block(p):
+        return pl.ds(STARTS[p] * n_seq, SIZES[p] * n_seq)
+
+    def z_copy(src, b, p, d):
+        return remote(src, raw.at[b, piece(p)], z_snd, z_rcv.at[b, p], mp=d)
+
+    def relayed(b, d):
+        return (((b == 1) & (d == 3)) | ((b == 2) & (d == 0))) & (RELAY == 1)
+
+    def plane_copy(src, b, p):
+        seq = jnp.where(b == c, mate, b * CORES + r)
+        lane_in = jnp.where(b == c, 1, 0)
+        return remote(src, xk.at[place(p, s)], k_snd, k_rcv.at[lane_in, p], seq=seq)
+
+    def z_send(p):
+        ups, downs = (range(n_mp - 1, 0, -1), range(n_mp - 1))
+        if NEAR:
+            ups, downs = (ups[::-1], downs[::-1])
+        for side, order in ((1, ups), (-1, downs)):
+            for d in order:
+
+                @pl.when(((d > m) if side > 0 else (d < m)) & jnp.logical_not(relayed(m, d)))
+                def _():
+                    z_copy(tok_ref.at[piece(p)], m, p, d).start()
+
+    def send_own(p):
+        plane_copy(tok_ref.at[piece(p)], m, p).start()
+
+        @pl.when(m == c)
+        def _():
+            xk[place(p, s), :] = tok_ref[piece(p), :]
+
+    def pass_on(p, k):
+        low = m < n_mp // 2
+        take(p, k, 1, low)
+        take(p, k, -1, True)
+        take(p, k, 1, jnp.logical_not(low))
+
+    def take(p, k, sign, when):
+        b = m + sign * k
+
+        @pl.when((b >= 0) & (b <= n_mp - 1) & when)
+        def _():
+            here = raw.at[b, piece(p)]
+            z_copy(here, b, p, m).wait_recv()
+            if k == 1 and RELAY:
+                far = n_mp - 1 if sign < 0 else 0
+
+                @pl.when(m == (n_mp - 2 if sign < 0 else 1))
+                def _():
+                    z_copy(here, b, p, far).start()
+
+            plane_copy(here, b, p).start()
+
+            @pl.when(b == c)
+            def _():
+                xk[place(p, s), :] = raw[b, piece(p), :]
+
+    z_send(0)
+    send_own(0)
     across = lax.broadcasted_iota(jnp.int32, (rows, rows), 0) == lax.broadcasted_iota(
         jnp.int32, (rows, rows), 1
     )
@@ -214,75 +298,11 @@
     squares = jnp.sum(wide * wide, axis=1, keepdims=True)
     squares = jnp.sum(jnp.where(across, squares, 0.0), axis=0, keepdims=True)
     sq_own[...] = jnp.broadcast_to(squares, sq_own.shape)
-    pl.semaphore_wait(pltpu.get_barrier_semaphore(), n_seq + n_mp - 2)
-
-    def piece(p):
-        return pl.ds(STARTS[p], SIZES[p])
-
-    def place(p, seq):
-        return pl.ds(pl.multiple_of(STARTS[p] * n_seq + seq * SIZES[p], SUBLANES * 2), SIZES[p])
-
-    def block(p):
-        return pl.ds(STARTS[p] * n_seq, SIZES[p] * n_seq)
-
-    def z_copy(src, b, p, d):
-        return remote(src, raw.at[b, piece(p)], z_snd, z_rcv.at[b, p], mp=d)
-
-    def relayed(b, d):
-        return ((b == 1) & (d == 3)) | ((b == 2) & (d == 0))
-
-    def plane_copy(src, b, p):
-        seq = jnp.where(b == c, mate, b * CORES + r)
-        lane_in = jnp.where(b == c, 1, 0)
-        return remote(src, xk.at[place(p, s)], k_snd, k_rcv.at[lane_in, p], seq=seq)
-
-    def z_send(p):
-        for d in range(n_mp - 1, 0, -1):
-
-            @pl.when((d > m) & jnp.logical_not(relayed(m, d)))
-            def _():
-                z_copy(tok_ref.at[piece(p)], m, p, d).start()
-
-        for d in range(n_mp - 1):
-
-            @pl.when((d < m) & jnp.logical_not(relayed(m, d)))
-            def _():
-                z_copy(tok_ref.at[piece(p)], m, p, d).start()
-
-    def send_own(p):
-        plane_copy(tok_ref.at[piece(p)], m, p).start()
-
-        @pl.when(m == c)
-        def _():
-            xk[place(p, s), :] = tok_ref[piece(p), :]
-
-    def pass_on(p, k):
-        for sign in (-1, 1):
-            b = m + sign * k
-
-            @pl.when((b >= 0) & (b <= n_mp - 1))
-            def _():
-                here = raw.at[b, piece(p)]
-                z_copy(here, b, p, m).wait_recv()
-                if k == 1:
-                    far = n_mp - 1 if sign < 0 else 0
-
-                    @pl.when(m == (n_mp - 2 if sign < 0 else 1))
-                    def _():
-                        z_copy(here, b, p, far).start()
-
-                plane_copy(here, b, p).start()
-
-                @pl.when(b == c)
-                def _():
-                    xk[place(p, s), :] = raw[b, piece(p), :]
-
     for o in range(1, n_mp):
-        copy = remote(sq_own, sq_all.at[o], q_snd, q_rcv, mp=(m + o) % n_mp)
-        copy.start()
-    for p in range(LOOK):
+        remote(sq_own, sq_all.at[o], q_snd, q_rcv, mp=(m + o) % n_mp).start()
+    for p in range(1, LOOK):
         z_send(p)
-    for p in range(OWN):
+    for p in range(1, OWN):
         send_own(p)
 
     w_out_copies = [
@@ -292,6 +312,8 @@
     ]
     for copy in w_out_copies:
         copy.start()
+    for copy in small:
+        copy.wait()
     wide_rows = width // LANES
     gain = jnp.concatenate([gain_ref[pl.ds(c * wide_rows + i, 1), :] for i in range(wide_rows)], axis=1)
     bias = bg_ref[pl.ds(q, 1), :]
@@ -306,7 +328,7 @@
             send_own(p + OWN)
         for k in range(1, n_mp):
             pass_on(p, k)
-            if p == 0 and k == 1:
+            if (p, k) == FACTORS_AT:
                 factors()
 
     def factors():
@@ -389,17 +411,17 @@
         sums(2, p, second).start()
 
     for turn in range(PIECES + CL + LAG):
-        if turn < PIECES:
-            stage_a(turn)
-        if turn == CL - 1:
-            spread_factors()
-            part = wk.at[pl.ds(0, n_chip // 2)]
-            pltpu.make_async_copy(part, part, w_loc).wait()
-            remote(part, part, w_snd, w_rcv, seq=s).wait_recv()
         if turn == WO_TURN:
             wo_copy.start()
         for what in ORDER:
+            if what == "a" and turn < PIECES:
+                stage_a(turn)
             if what == "c" and 0 <= turn - CL < PIECES:
+                if turn == CL:
+                    spread_factors()
+                    part = wk.at[pl.ds(0, n_chip // 2)]
+                    pltpu.make_async_copy(part, part, w_loc).wait()
+                    remote(part, part, w_snd, w_rcv, seq=s).wait_recv()
                 stage_c(turn - CL)
             if what == "b" and 0 <= turn - BL < PIECES:
                 stage_b(turn - BL)
@@ -552,10 +574,14 @@
     return pl.pallas_call(
         functools.partial(fused_kernel, n_seq, n_mp),
         out_shape=pltpu.VMEM((rows, width), bf16),
-        in_specs=[far, whole, far, far, whole, whole, whole, far],
+        in_specs=[far] * 8,
         out_specs=whole,
         scratch_shapes=[
             vmem((rows, width), bf16),
+            vmem((n_mp * width // LANES, LANES), f32),
+            vmem((n_seq, LANES), f32),
+            vmem((n_seq, LANES), f32),
+            vmem((n_seq, LANES), f32),
             vmem((n_mp, rows, width), bf16),
             vmem((length, width), bf16),
             vmem((length * max(SIZES) // sum(SIZES), width), bf16),
@@ -585,6 +611,7 @@
             dma,
             dma,
             dma,
+            dma((4,)),
             dma,
             dma((n_mp, PIECES)),
             dma,

time: 74 us -> 71.3 us (0.964)
  Pallas kernels: 73.1 us -> 70.4 us
    pallas_call x1, Pallas kernels: 73.1 us -> 70.4 us  [fused(): pl.pallas_call(functools.partial(fused_kernel, n_seq, n_mp), out_shape=pl...]
where the time goes in v2:
time: 71.3 us; the launch traced here: 71.1 us
  Pallas kernels  70.4 us (99%)
    pallas_call x1, Pallas kernels, fused(): pl.pallas_call(functools.partial(fused_kernel, n_seq, n_mp), out_shape=pl...  70.4 us

profile of v2, /device:TPU:0, one launch (start us, length us, event | category | flops | bytes accessed | tf_op | source)
XLA Modules:
  0.0 71.1 jit_solution(8203560632137842833)
XLA Ops:
  0.0 70.4 %shard_map.82 = bf16[128,1024]{1,0:T(8,128)(2,1)S(1)} custom-call(bf16[128,1024]{1,0:T(8,128)(2,1)} %tok_hbm.1, f32[32,128]{1,0:T(8,128)} %bitcast.4, bf16[512,1024]{1,0:T(8,128)(2,1)} %wc_hbm.1, bf16[512,1024]{1,0:T(8,128)(2,1)} %wg_hbm.1, f32[8,128]{1,0:T(8,128)} %bitcast.5, f32[8,128]{1,0:T(8,128)} %bitcast.6, f32[8,128]{1,0:T(8,128)} %bitcast.7, ...), custom_call_target="tpu_custom_call" | custom-call | tf_op jit(solution)/shard_map/pallas_call | solution.py:574
  70.4 0.7 copy.10

commit v3 on v2

--- a/solution.py
+++ b/solution.py
@@ -93,7 +93,7 @@
 CORES = 2
 SUBLANES = 8
 LANES = 128
-SIZES = (16, 16, 32, 32, 32)
+SIZES = (16, 16, 32, 32, 16, 16)
 PIECES = len(SIZES)
 STARTS = tuple(sum(SIZES[:i]) for i in range(PIECES))
 HALVES = 2
@@ -102,7 +102,7 @@
 FACTORS_AT = (0, 2)
 LAG = 2
 LOOK = 2
-WO_TURN = 5
+WO_TURN = 6
 UNROLL = 4
 OWN = 1
 BL = 1
@@ -380,35 +380,44 @@
         def product(chip):
             return jnp.dot(xn[:tile, :], wk[chip], preferred_element_type=jnp.float32)
 
-        at = block(p)
-        first, second = ends(p)
-        psend[1, at, :] = product(n_chip - 1 - c).astype(jnp.bfloat16)
-        sums(1, p, first).start()
-        psend[0, at, :] = product(first).astype(jnp.bfloat16)
-        sums(0, p, first).start()
-        onward[at, :] = product(second)
-        own[at, :] = product(c)
-
-    def ends(p):
-        beside, above = (c + 1 - 2 * (c % 2), (c + n_chip // 2) % n_chip)
-        return (beside, above) if p % 2 == 0 else (above, beside)
-
-    def sums(slot, p, chip):
-        at = block(p)
+        beside, above = near
+        mid = tile // 2
+        psend[1, block(p), :] = product(n_chip - 1 - c).astype(jnp.bfloat16)
+        sums(1, p, 0, beside).start()
+        sums(1, p, 1, above).start()
+        value = product(beside)
+        psend[0, split(p, 0), :] = value[:mid].astype(jnp.bfloat16)
+        onward[split(p, 1), :] = value[mid:]
+        sums(0, p, 0, beside).start()
+        value = product(above)
+        psend[0, split(p, 1), :] = value[mid:].astype(jnp.bfloat16)
+        onward[split(p, 0), :] = value[:mid]
+        sums(0, p, 1, above).start()
+        own[block(p), :] = product(c)
+
+    near = (c + 1 - 2 * (c % 2), (c + n_chip // 2) % n_chip)
+
+    def split(p, h):
+        mid = SIZES[p] * n_seq // 2
+        return pl.ds(STARTS[p] * n_seq + h * mid, mid)
+
+    def sums(slot, p, h, chip):
+        at = split(p, h)
         return remote(
-            psend.at[slot, at], precv.at[slot, at], p_snd, p_rcv.at[int(slot != 1), p], seq=chip * CORES + r
+            psend.at[slot, at], precv.at[slot, at], p_snd, p_rcv.at[h if slot == 1 else 2, p], seq=chip * CORES + r
         )
 
     def stage_d(p):
-        _, second = ends(p)
-        sums(1, p, second).wait_recv()
-
-        @pl.loop(0, SIZES[p] * n_seq // GROUP)
-        def _(i):
-            at = pl.ds(pl.multiple_of(STARTS[p] * n_seq + i * GROUP, GROUP), GROUP)
-            psend[2, at, :] = (onward[at, :] + precv[1, at, :].astype(jnp.float32)).astype(jnp.bfloat16)
-
-        sums(2, p, second).start()
+        for h in range(2):
+            sums(1, p, h, near[h]).wait_recv()
+            mid = SIZES[p] * n_seq // 2
+
+            @pl.loop(0, mid // GROUP)
+            def _(i):
+                at = pl.ds(pl.multiple_of(STARTS[p] * n_seq + h * mid + i * GROUP, GROUP), GROUP)
+                psend[2, at, :] = (onward[at, :] + precv[1, at, :].astype(jnp.float32)).astype(jnp.bfloat16)
+
+            sums(2, p, h, near[1 - h]).start()
 
     for turn in range(PIECES + CL + LAG):
         if turn == WO_TURN:
@@ -430,7 +439,7 @@
 
     def gather_piece(p):
         both = precv.at[pl.ds(0, 2), block(p)]
-        remote(both, both, p_snd, p_rcv.at[1, p], seq=s).wait_recv()
+        remote(both, both, p_snd, p_rcv.at[2, p], seq=s).wait_recv()
 
         @pl.loop(0, SIZES[p] * n_seq // GROUP)
         def _(i):
@@ -622,7 +631,7 @@
             dma,
             dma,
             dma,
-            dma((2, PIECES)),
+            dma((3, PIECES)),
             dma,
             dma,
             dma,

time: 71.3 us -> 70.2 us (0.985)
  Pallas kernels: 70.4 us -> 69.3 us
    pallas_call x1, Pallas kernels: 70.4 us -> 69.3 us  [fused(): pl.pallas_call(functools.partial(fused_kernel, n_seq, n_mp), out_shape=pl...]
where the time goes in v3:
time: 70.2 us; the launch traced here: 70 us
  Pallas kernels  69.3 us (99%)
  local copies, waits for them, and re-layouts  0.71 us (1%)
    pallas_call x1, Pallas kernels, fused(): pl.pallas_call(functools.partial(fused_kernel, n_seq, n_mp), out_shape=pl...  69.3 us

profile of v3, /device:TPU:0, one launch (start us, length us, event | category | flops | bytes accessed | tf_op | source)
XLA Modules:
  0.0 70.0 jit_solution(9489695518918241165)
XLA Ops:
  0.0 69.3 %shard_map.82 = bf16[128,1024]{1,0:T(8,128)(2,1)S(1)} custom-call(bf16[128,1024]{1,0:T(8,128)(2,1)} %tok_hbm.1, f32[32,128]{1,0:T(8,128)} %bitcast.4, bf16[512,1024]{1,0:T(8,128)(2,1)} %wc_hbm.1, bf16[512,1024]{1,0:T(8,128)(2,1)} %wg_hbm.1, f32[8,128]{1,0:T(8,128)} %bitcast.5, f32[8,128]{1,0:T(8,128)} %bitcast.6, f32[8,128]{1,0:T(8,128)} %bitcast.7, ...), custom_call_target="tpu_custom_call" | custom-call | tf_op jit(solution)/shard_map/pallas_call | solution.py:583
  69.3 0.7 %copy.10 = bf16[128,1024]{1,0:T(8,128)(2,1)} copy(bf16[128,1024]{1,0:T(8,128)(2,1)S(1)} %shard_map.82) | data formatting | bytes 524288

commit v4 on v3

--- a/solution.py
+++ b/solution.py
@@ -484,15 +484,17 @@
             j = STARTS[p] + i
             cand_n[pl.ds(STARTS[p] * n_seq + i, n_seq, stride=SIZES[p]), :] = sweep_a[j] * entering + sweep_b[j]
 
-    for i in range(n_seq):
+    def rounded(seq):
         for p in range(PIECES):
-            start, size = STARTS[p] * n_seq + i * SIZES[p], SIZES[p]
-            ssend[i, piece(p), :] = cand_n[start : start + size, :].astype(jnp.bfloat16)
+            ssend[pl.ds(seq, 1), piece(p), :] = cand_n[place(p, seq), :].astype(jnp.bfloat16)[None]
+
     lane = pl.ds(pl.multiple_of(q * LANES, LANES), LANES)
     for o in range(1, n_seq):
         there = (s + o) % n_seq
+        rounded(there)
         copy = remote(ssend.at[there], sall.at[:, lane], s_snd, s_rcv, seq=there)
         copy.start()
+    rounded(s)
     sall[:, lane] = ssend[pl.ds(s, 1)].reshape(rows, LANES)
     def sent(ref, sem):
         remote(ref, ref, sem, s_rcv, seq=s).wait_send()

time: 70.2 us -> 70.2 us (level)
  no operation moved by 1% of the time
where the time goes in v4:
time: 70.2 us; the launch traced here: 70 us
  Pallas kernels  69.3 us (99%)
  local copies, waits for them, and re-layouts  0.71 us (1%)
    pallas_call x1, Pallas kernels, fused(): pl.pallas_call(functools.partial(fused_kernel, n_seq, n_mp), out_shape=pl...  69.3 us

profile of v4, /device:TPU:0, one launch (start us, length us, event | category | flops | bytes accessed | tf_op | source)
XLA Modules:
  0.0 70.0 jit_solution(17638849098342953199)
XLA Ops:
  0.0 69.3 %shard_map.82 = bf16[128,1024]{1,0:T(8,128)(2,1)S(1)} custom-call(bf16[128,1024]{1,0:T(8,128)(2,1)} %tok_hbm.1, f32[32,128]{1,0:T(8,128)} %bitcast.4, bf16[512,1024]{1,0:T(8,128)(2,1)} %wc_hbm.1, bf16[512,1024]{1,0:T(8,128)(2,1)} %wg_hbm.1, f32[8,128]{1,0:T(8,128)} %bitcast.5, f32[8,128]{1,0:T(8,128)} %bitcast.6, f32[8,128]{1,0:T(8,128)} %bitcast.7, ...), custom_call_target="tpu_custom_call" | custom-call | tf_op jit(solution)/shard_map/pallas_call | solution.py:585
  69.3 0.7 %copy.10 = bf16[128,1024]{1,0:T(8,128)(2,1)} copy(bf16[128,1024]{1,0:T(8,128)(2,1)S(1)} %shard_map.82) | data formatting | bytes 524288
